TPU v7x, 32 devices: a whole 2x2x4 slice. The times are simulated.
32 devices in a mesh: group: 2 (over x), expert: 16 (over z, y, core).
Axes of the slice: x: 2, y: 2, z: 4, core: 2. Of those that a mesh axis runs over, the one named last changes fastest.
Arguments:
- hidden: bfloat16 [4096, 4096], P(('group', 'expert')), parts along dimension 0, may hold values from -6 to 6
- norm_gain: bfloat16 [4096], replicated, may hold values from 0.25 to 1.75
- router_weight: bfloat16 [4096, 128], replicated, may hold values from -0.03125 to 0.03125
- expert_ids: int32 [4096, 8], P(('group', 'expert')), parts along dimension 0, may hold values from 0 to 127, all different within a row; in each aligned block of 128 rows (0 to 127, 128 to 255, ...) at most 16 rows name the same one
- gate_weight: bfloat16 [16, 4096, 384], P('expert'), may hold values from -0.09375 to 0.09375
- up_weight: bfloat16 [16, 4096, 384], P('expert'), may hold values from -0.09375 to 0.09375
- down_weight: bfloat16 [16, 384, 4096], P('expert'), may hold values from -0.625 to 0.625
Outputs:
- moe_out: bfloat16 [4096, 4096], P(('group', 'expert')), parts along dimension 0
There are 2 independent parts, one for each index of `group`. A program takes and returns all parts, laid end to end along the dimension named above; an argument that names none is the same for every part. Nothing has to cross between parts.
Inputs may be any that keep to these rules, and one draw needn't show every extreme that they name: `expert_ids`: each row names 8 different experts; in each aligned block of 128 rows (the rows of one device) no expert is named by more than 16 rows.
All inputs are finite; a program needn't handle non-finite values.
Results may differ from a plain program's by a relative error of at most 0.0077.
Values may be sent and summed in bfloat16 or wider, within the bound.
A program may use at most 128 MiB of HBM per device.

v0:
```python
import jax
import jax.numpy as jnp
from jax import lax
from jax.sharding import PartitionSpec as P

SPLIT = 4
CAP = 16


def expert_rows(row_block, gate_weight, up_weight, down_weight):
    gate_act = jnp.dot(row_block, gate_weight[0], preferred_element_type=jnp.float32)
    up_act = jnp.dot(row_block, up_weight[0], preferred_element_type=jnp.float32)
    hidden_act = (jax.nn.silu(gate_act) * up_act).astype(jnp.bfloat16)
    return jnp.dot(hidden_act, down_weight[0], preferred_element_type=jnp.float32).astype(
        jnp.bfloat16
    )


def shards(hidden, norm_gain, router_weight, expert_ids, gate_weight, up_weight, down_weight):
    devices = lax.axis_size("expert")
    flight = devices // SPLIT
    tok_rows = hidden.shape[0]
    model_width = hidden.shape[1]
    pick_count = expert_ids.shape[1]
    widened = hidden.astype(jnp.float32)
    inv_rms = lax.rsqrt(jnp.mean(widened * widened, axis=-1, keepdims=True) + 1e-06)
    normed = (widened * inv_rms * norm_gain.astype(jnp.float32)).astype(jnp.bfloat16)
    logits = jnp.dot(normed, router_weight, preferred_element_type=jnp.float32)
    router_probs = jax.nn.softmax(logits, axis=-1)
    picked = jnp.take_along_axis(router_probs, expert_ids, axis=1)
    gate_share = picked / jnp.sum(picked, axis=1, keepdims=True)
    flat_ids = expert_ids.reshape(-1)
    onehot = (flat_ids[:, None] == jnp.arange(flight, dtype=jnp.int32)[None, :]).astype(jnp.int32)
    before = jnp.cumsum(onehot, axis=0) - onehot
    slot_index = jnp.sum(before * onehot, axis=1)
    is_live = jnp.sum(onehot, axis=1) > 0
    owner = jnp.where(is_live, flat_ids, 0)
    column = owner * CAP + slot_index
    select = (column[:, None] == jnp.arange(flight * CAP, dtype=jnp.int32)[None, :]) & is_live[
        :, None
    ]
    select = select.reshape(tok_rows, pick_count, flight * CAP)
    dispatch = jnp.any(select, axis=1).astype(jnp.bfloat16)
    outgoing = jnp.einsum("tc,td->cd", dispatch, normed, preferred_element_type=jnp.float32).astype(
        jnp.bfloat16
    )
    sending = jnp.tile(outgoing.reshape(flight, CAP, model_width), (SPLIT, 1, 1))
    arrived = lax.all_to_all(sending, "expert", split_axis=0, concat_axis=0, tiled=True)
    row_count = arrived.shape[1]
    partial_value = expert_rows(
        arrived.reshape(-1, model_width), gate_weight, up_weight, down_weight
    )
    partial_value = partial_value.reshape(devices, row_count, model_width)
    returned = lax.all_to_all(partial_value, "expert", split_axis=0, concat_axis=0, tiled=True)
    summed = jnp.sum(
        returned.reshape(SPLIT, flight, row_count, model_width).astype(jnp.float32), axis=0
    )
    results = summed.astype(jnp.bfloat16)
    results = results.reshape(flight * CAP, model_width)
    pick_rows = jnp.take(results, column, axis=0).reshape(tok_rows, pick_count, model_width)
    pick_weight = jnp.where(is_live, gate_share.reshape(-1), 0.0).reshape(tok_rows, pick_count)
    moe_out = jnp.zeros((tok_rows, model_width), jnp.float32)
    for pick in range(pick_count):
        moe_out = moe_out + pick_weight[:, pick][:, None] * pick_rows[:, pick].astype(jnp.float32)
    return moe_out.astype(jnp.bfloat16)


def solution(mesh):
    in_specs = (
        P(("group", "expert"), None),
        P(),
        P(),
        P(("group", "expert"), None),
        P("expert", None, None),
        P("expert", None, None),
        P("expert", None, None),
    )
    out_specs = P(("group", "expert"), None)
    return jax.shard_map(shards, mesh=mesh, in_specs=in_specs, out_specs=out_specs, check_vma=False)
```

profile of v0, /device:TPU:13, one launch (start us, length us, event | category | flops | bytes accessed | tf_op | source)
XLA Modules:
  0.0 165.0 jit_solution(15530889888116270357)
XLA Ops:
  0.0 0.9 copy.46
  0.9 0.1 eq.43
  1.0 0.1 eq.39
  1.1 1.5 fusion.5
  2.7 0.7 convert_element_type.81
  3.4 1.1 reduce-window.6
  4.5 0.2 slice_reduce_fusion
  4.7 0.2 reduce-window.9
  4.9 0.1 add_bitcast_fusion
  5.0 0.1 gt.35
  5.1 0.1 copy.49
  5.2 0.1 reduce_sum.66
  5.3 0.7 compare_and_fusion
  6.1 1.7 %convolution_convert_fusion.1 = bf16[64,4096]{1,0:T(8,128)(2,1)S(1)} fusion(pred[128,64]{0,1:T(8,128)(4,1)S(1)} %fusion.33, bf16[128,4096]{1,0:T(8,128)(2,1)} %param.7, f32[4096]{0:T(1024)S(1)} %convert_element_type.81, f32[128]{0:T(128)S(1)} %add_rsqrt_fusion), kind=kOutput, calls=%fused_computation.4 | convolution fusion | flops 69468160 | bytes 1597952 | tf_op jit(solution)/shard_map/tc,td->cd/dot_general | solution.py:44
  7.8 0.2 tile.11
  8.1 0.0 copy-start.3
  8.1 53.9 %all_to_all.10 = bf16[16,16,4096]{2,1,0:T(8,128)(2,1)S(1)} all-to-all(bf16[16,16,4096]{2,1,0:T(8,128)(2,1)S(1)} %bitcast.101), channel_id=1, replica_groups=mesh['group'=2,'expert'=16] {'expert'}, dimensions={0} | all-to-all | bytes 4194304 | tf_op jit(solution)/shard_map/all_to_all | solution.py:48
  62.0 1.3 copy-done.1
  63.3 2.1 %fusion.3 = f32[256,384]{1,0:T(8,128)} fusion(bf16[256,4096]{1,0:T(8,128)(2,1)S(1)} %bitcast.103, bf16[1,4096,384]{2,1,0:T(8,128)(2,1)S(1)} %copy-done.3), kind=kOutput, calls=%fused_computation.8 | convolution fusion | flops 805306368 | bytes 5636096 | tf_op jit(solution)/shard_map/dot_general | solution.py:11
  65.4 6.4 %convolution_convert_fusion = bf16[256,4096]{1,0:T(8,128)(2,1)} fusion(bf16[1,384,4096]{2,1,0:T(8,128)(2,1)S(1)} %copy-done, bf16[256,4096]{1,0:T(8,128)(2,1)} %bitcast.104, bf16[1,4096,384]{2,1,0:T(8,128)(2,1)} %param.12, f32[256,384]{1,0:T(8,128)} %fusion.3), kind=kOutput, calls=%fused_computation.3 | convolution fusion | flops 1612251136 | bytes 10878976 | tf_op jit(solution)/shard_map/dot_general | solution.py:14
  71.7 5.2 %all-to-all-start.1 = ((bf16[16,16,4096]{2,1,0:T(8,128)(2,1)}), bf16[16,16,4096]{2,1,0:T(8,128)(2,1)}, u32[]{:S(2)}, u32[]{:S(2)}) async-start(bf16[16,16,4096]{2,1,0:T(8,128)(2,1)} %bitcast.102), calls=%async_computation.1 | async-start | bytes 4194304 | tf_op jit(solution)/shard_map/all_to_all | solution.py:54
  76.9 0.1 reshape.168
  77.0 0.1 copy.47
  77.1 0.1 reshape.185
  77.2 2.2 %fusion.44 = (f32[128]{0:T(128)S(1)}, f32[128,128]{0,1:T(8,128)S(1)}) fusion(bf16[4096,128]{1,0:T(8,128)(2,1)} %param.9, bf16[128,4096]{1,0:T(8,128)(2,1)} %param.7, f32[4096]{0:T(1024)S(1)} %convert_element_type.81, f32[128]{0:T(128)S(1)} %add_rsqrt_fusion), kind=kOutput, calls=%fused_computation.88 | convolution fusion | flops 136331136 | bytes 2180096 | tf_op jit(solution)/shard_map/dot_general | solution.py:28
  79.4 7.0 %gather_fusion.1 = f32[1024]{0:T(1024)S(1)} fusion(f32[128,128]{0,1:T(8,128)S(1)} %fusion.35, s32[1024]{0:T(1024)S(1)} %reshape.185), kind=kCustom, calls=%fused_computation.1 | custom fusion | bytes 16384 | tf_op jit(solution)/shard_map/jit(take_along_axis)/gather | solution.py:30
  86.5 0.1 reshape.188
  86.7 37.7 %all-to-all-done.1 = bf16[16,16,4096]{2,1,0:T(8,128)(2,1)} async-done(((bf16[16,16,4096]{2,1,0:T(8,128)(2,1)}), bf16[16,16,4096]{2,1,0:T(8,128)(2,1)}, u32[]{:S(2)}, u32[]{:S(2)}) %all-to-all-start.1) | async-done | bytes 2097184 | tf_op jit(solution)/shard_map/all_to_all | solution.py:54
  124.4 2.9 %reduce_sum.67 = bf16[4,16,4096]{2,1,0:T(8,128)(2,1)} reduce(bf16[4,4,16,4096]{3,2,1,0:T(8,128)(2,1)} %bitcast.10, bf16[]{:T(256)} %constant.54.clone.1), dimensions={0}, to_apply=%region_9.10 | reduce | flops 786432 | bytes 2621442 | tf_op jit(solution)/shard_map/reduce_sum | solution.py:55
  127.3 16.2 %gather_fusion = bf16[1024,4096]{1,0:T(8,128)(2,1)} fusion(bf16[64,4096]{1,0:T(8,128)(2,1)} %bitcast.99, s32[1024]{0:T(1024)S(1)} %broadcast_clamp_fusion), kind=kCustom, calls=%fused_computation | custom fusion | bytes 16781312 | tf_op jit(solution)/shard_map/jit(_take)/gather | solution.py:60
  143.4 16.3 %copy_select_fusion = bf16[128,8,4096]{2,0,1:T(8,128)(2,1)} fusion(bf16[128,8,4096]{2,1,0:T(8,128)(2,1)} %bitcast.100, pred[128,8]{0,1:T(8,128)(4,1)S(1)} %get-tuple-element.7), kind=kLoop, calls=%fused_computation.2 | loop fusion | flops 4194304 | bytes 16778240 | tf_op jit(solution)/shard_map/jit(_take)/select_n | solution.py:60
  159.8 5.3 %fusion.9 = bf16[128,4096]{1,0:T(8,128)(2,1)} fusion(bf16[128,8,4096]{2,0,1:T(8,128)(2,1)} %copy_select_fusion, f32[128]{0:T(128)S(1)} %get-tuple-element.10, f32[128]{0:T(128)S(1)} %get-tuple-element.11, f32[128]{0:T(128)S(1)} %get-tuple-element.12, f32[128]{0:T(128)S(1)} %get-tuple-element.13, f32[128]{0:T(128)S(1)} %get-tuple-element.14, ...), kind=kLoop, calls=%fused_computation.17 | loop fusion | flops 12582912 | bytes 9441280 | tf_op jit(solution)/shard_map/convert_element_type | solution.py:65
  (21 shorter events, 0.3 us)
Async XLA Ops:
  0.0 65.4 %copy-start = (bf16[1,384,4096]{2,1,0:T(8,128)(2,1)S(1)}, bf16[1,384,4096]{2,1,0:T(8,128)(2,1)}, u32[]{:S(2)}) copy-start(bf16[1,384,4096]{2,1,0:T(8,128)(2,1)} %param.13) | copy-start | bytes 9437188
  8.1 55.2 %copy-start.3 = (bf16[1,4096,384]{2,1,0:T(8,128)(2,1)S(1)}, bf16[1,4096,384]{2,1,0:T(8,128)(2,1)}, u32[]{:S(2)}) copy-start(bf16[1,4096,384]{2,1,0:T(8,128)(2,1)} %param.11) | copy-start | bytes 9437188
  62.0 1.3 copy-start.1
  71.7 5.3 %copy-start.2 = (s32[128,8]{0,1:T(8,128)S(1)}, s32[128,8]{0,1:T(8,128)}, u32[]{:S(2)}) copy-start(s32[128,8]{0,1:T(8,128)} %param.10) | copy-start | bytes 12292
  71.7 52.7 %all-to-all-start.1 = ((bf16[16,16,4096]{2,1,0:T(8,128)(2,1)}), bf16[16,16,4096]{2,1,0:T(8,128)(2,1)}, u32[]{:S(2)}, u32[]{:S(2)}) async-start(bf16[16,16,4096]{2,1,0:T(8,128)(2,1)} %bitcast.102), calls=%async_computation.1 | async-start | bytes 4194304 | tf_op jit(solution)/shard_map/all_to_all | solution.py:54
where the time goes:
time: 166 us; the launch traced here: 165 us
  blocking collectives  53.9 us (32%)
  waiting for transfers between devices  37.7 us (23%)
  other arithmetic  29 us (17%)
  local copies, waits for them, and re-layouts  26.8 us (16%)
  matrix products  12.3 us (7%)
  starting transfers between devices  5.16 us (3%)
    all_to_all x1, blocking collectives, shards(): lax.all_to_all(sending, 'expert', split_axis=0, concat_axis=0, tiled=True)  53.9 us
    all_to_all x1, waiting for transfers between devices, shards(): lax.all_to_all(partial_value, 'expert', split_axis=0, concat_axis=0, tile...  37.7 us
    select_n x2, other arithmetic, shards(): jnp.take(results, column, axis=0).reshape(tok_rows, pick_count, model_width)  16.4 us
    gather x1, local copies, waits for them, and re-layouts, shards(): jnp.take(results, column, axis=0).reshape(tok_rows, pick_count, model_width)  16.2 us
    gather x5, local copies, waits for them, and re-layouts, shards(): picked = jnp.take_along_axis(router_probs, expert_ids, axis=1)  7.34 us
    dot_general x1, matrix products, expert_rows(): jnp.dot(hidden_act, down_weight[0], preferred_element_type=jnp.float32)  6.36 us
    convert_element_type x1, other arithmetic, shards(): return moe_out.astype(jnp.bfloat16)  5.26 us
    all_to_all x1, starting transfers between devices, shards(): lax.all_to_all(partial_value, 'expert', split_axis=0, concat_axis=0, tile...  5.16 us
  transfers between devices with their start and end apart: 1, of which 1 were waited for; matrix products, arithmetic and copies ran while one was open for 6% of the time, Pallas kernels for 0%

commit v1 on v0

v1 whole, which is shorter than its diff:
```python
import functools

import jax
import jax.numpy as jnp
from jax import lax
from jax.experimental import pallas as pl
from jax.experimental.pallas import tpu as pltpu
from jax.sharding import PartitionSpec as P

SPLIT = 4
CAP = 16
F32 = jnp.float32
BF16 = jnp.bfloat16


def route_kernel(flight, hidden_ref, gain_ref, router_ref, ids_ref, out_ref, hi_ref, lo_ref):
    rows = hidden_ref.shape[0]
    experts = router_ref.shape[1]
    cols = flight * CAP
    widened = hidden_ref[...].astype(F32)
    inv_rms = lax.rsqrt(jnp.mean(widened * widened, axis=-1, keepdims=True) + 1e-06)
    normed = (widened * inv_rms * gain_ref[...].astype(F32)).astype(BF16)
    logits = jnp.dot(normed, router_ref[...], preferred_element_type=F32)
    shifted = jnp.exp(logits - jnp.max(logits, axis=-1, keepdims=True))
    probs = shifted / jnp.sum(shifted, axis=-1, keepdims=True)
    ids = ids_ref[...]
    expert = lax.broadcasted_iota(jnp.int32, (rows, experts), 1)
    chosen = jnp.zeros((rows, experts), F32)
    for k in range(ids.shape[1]):
        chosen = jnp.where(ids[:, k : k + 1] == expert, 1.0, chosen)
    picked = probs * chosen
    share = picked / jnp.sum(picked, axis=-1, keepdims=True)
    chosen_b = chosen.astype(BF16)
    earlier = lax.broadcasted_iota(jnp.int32, (rows, rows), 1) < lax.broadcasted_iota(
        jnp.int32, (rows, rows), 0
    )
    slot = jnp.dot(jnp.where(earlier, 1.0, 0.0).astype(BF16), chosen_b, preferred_element_type=F32)
    spread = (
        lax.broadcasted_iota(jnp.int32, (experts, cols), 1) // CAP
        == lax.broadcasted_iota(jnp.int32, (experts, cols), 0)
    )
    spread = jnp.where(spread, 1.0, 0.0).astype(BF16)
    slot_of = jnp.dot(slot.astype(BF16), spread, preferred_element_type=F32)
    live_of = jnp.dot(chosen_b, spread, preferred_element_type=F32)
    share_hi = share.astype(BF16)
    share_lo = (share - share_hi.astype(F32)).astype(BF16)
    hi_of = jnp.dot(share_hi, spread, preferred_element_type=F32)
    lo_of = jnp.dot(share_lo, spread, preferred_element_type=F32)
    place = (lax.broadcasted_iota(jnp.int32, (rows, cols), 1) % CAP).astype(F32)
    select = (live_of > 0.5) & (slot_of == place)
    hi_ref[...] = jnp.where(select, hi_of, 0.0).astype(BF16)
    lo_ref[...] = jnp.where(select, lo_of, 0.0).astype(BF16)
    dispatch = jnp.where(select, 1.0, 0.0).astype(BF16)
    out_ref[...] = lax.dot_general(
        dispatch, normed, (((0,), (0,)), ((), ())), preferred_element_type=F32
    ).astype(BF16)


def expert_kernel(
    flight,
    out_ref,
    hi_ref,
    lo_ref,
    gate_hbm,
    up_hbm,
    down_hbm,
    moe_ref,
    gate_v,
    up_v,
    down_v,
    act_v,
    x_v,
    p_v,
    r_v,
    res_v,
    w_sem,
    own_sem,
    p1_send,
    p1_recv,
    ag_send,
    ag_recv,
    rs_send,
    rs_recv,
    ret_send,
    ret_recv,
):
    dev = lax.axis_index("expert")
    m = dev // flight
    e = dev % flight
    last = SPLIT - 1
    width = out_ref.shape[1]
    tile = min(512, width)

    weights = [
        pltpu.make_async_copy(gate_hbm.at[0], gate_v, w_sem.at[0]),
        pltpu.make_async_copy(up_hbm.at[0], up_v, w_sem.at[1]),
        pltpu.make_async_copy(down_hbm.at[0], down_v, w_sem.at[2]),
    ]
    for copy in weights:
        copy.start()

    def band(c):
        return pl.ds(pl.multiple_of(c * CAP, CAP), CAP)

    def remote(src, dst, ssem, rsem, target):
        return pltpu.make_async_remote_copy(
            src_ref=src,
            dst_ref=dst,
            send_sem=ssem,
            recv_sem=rsem,
            device_id={"expert": target},
            device_id_type=pl.DeviceIdType.MESH,
        )

    def mate(j):
        return (e + j) % flight

    barrier = pltpu.get_barrier_semaphore()

    def greet(target):
        pl.semaphore_signal(
            barrier, inc=1, device_id={"expert": target}, device_id_type=pl.DeviceIdType.MESH
        )

    @pl.loop(1, flight)
    def _(j):
        greet(m * flight + mate(j))

    @pl.when(m > 0)
    def _():
        greet(dev - flight)

    @pl.when(m < last)
    def _():
        greet(dev + flight)

    pl.semaphore_wait(
        barrier, flight - 1 + jnp.where(m > 0, 1, 0) + jnp.where(m < last, 1, 0)
    )

    def first(j):
        c = mate(j)
        return remote(
            out_ref.at[band(c)],
            x_v.at[m, band(e)],
            p1_send.at[c],
            p1_recv.at[e],
            m * flight + c,
        )

    def first_arrival(c):
        return remote(out_ref.at[band(c)], x_v.at[m, band(c)], p1_send.at[c], p1_recv.at[c], dev)

    own = pltpu.make_async_copy(out_ref.at[band(e)], x_v.at[m, band(e)], own_sem.at[0])
    own.start()

    @pl.loop(1, flight)
    def _(j):
        first(j).start()

    def pass_on(s, c, up):
        target = dev + flight if up else dev - flight
        return remote(
            x_v.at[s, band(c)],
            x_v.at[s, band(c)],
            ag_send.at[1 if up else 0, s, c],
            ag_recv.at[s, c],
            target,
        )

    def spread(s, c):
        @pl.when((m < last) & (s <= m))
        def _():
            pass_on(s, c, True).start()

        @pl.when((m > 0) & (s >= m))
        def _():
            pass_on(s, c, False).start()

    own.wait()
    spread(m, e)

    @pl.loop(1, flight)
    def _(j):
        c = mate(flight - j)
        first_arrival(c).wait_recv()
        spread(m, c)

    for copy in weights:
        copy.wait()

    def give(s, c, up):
        if up:
            target = dev + flight
            slot = jnp.where(s == m + 1, SPLIT, s)
        else:
            target = dev - flight
            slot = s
        return remote(
            p_v.at[s, band(c)], r_v.at[slot, band(c)], rs_send.at[s, c], rs_recv.at[slot, c], target
        )

    def taken(slot, c):
        return remote(
            r_v.at[slot, band(c)], r_v.at[slot, band(c)], rs_send.at[0, c], rs_recv.at[slot, c], dev
        )

    def compute(s):
        rows = x_v[s]
        gate = jnp.dot(rows, gate_v[...], preferred_element_type=F32)
        up = jnp.dot(rows, up_v[...], preferred_element_type=F32)
        act_v[...] = (jax.nn.silu(gate) * up).astype(BF16)

        @pl.loop(0, width // tile)
        def _(i):
            at = pl.ds(pl.multiple_of(i * tile, tile), tile)
            p_v[s, :, at] = jnp.dot(
                act_v[...], down_v[:, at], preferred_element_type=F32
            ).astype(BF16)

    @pl.loop(0, SPLIT)
    def _(t):
        @pl.loop(0, 2)
        def _(d):
            s = jnp.where(d == 0, m - t, m + t)

            @pl.when((t > 0) & (s >= 0) & (s <= last))
            def _():
                @pl.loop(0, flight)
                def _(c):
                    pass_on(s, c, True).wait_recv()
                    spread(s, c)

        @pl.loop(0, 2)
        def _(d):
            s = jnp.where(d == 0, m - t, m + t)

            @pl.when((s >= 0) & (s <= last) & ((t > 0) | (d == 0)))
            def _():
                compute(s)

                @pl.when((s < m) & (m == last))
                def _():
                    @pl.loop(0, flight)
                    def _(c):
                        give(s, c, False).start()

                @pl.when((s > m) & (m == 0))
                def _():
                    @pl.loop(0, flight)
                    def _(c):
                        give(s, c, True).start()

    def add(s, slot, c):
        taken(slot, c).wait_recv()
        p_v[s, band(c), :] = (
            p_v[s, band(c), :].astype(F32) + r_v[slot, band(c), :].astype(F32)
        ).astype(BF16)

    @pl.loop(3, 2 * last)
    def _(due):
        fall = 2 * last - m - due
        rise = due - m

        @pl.when((fall >= 0) & (fall < m) & (m < last))
        def _():
            @pl.loop(0, flight)
            def _(c):
                add(fall, fall, c)
                give(fall, c, False).start()

        @pl.when((rise <= last) & (rise > m) & (m > 0))
        def _():
            @pl.loop(0, flight)
            def _(c):
                add(rise, rise, c)
                give(rise, c, True).start()

    def back(c):
        return remote(
            p_v.at[m, band(c)],
            res_v.at[band(e)],
            ret_send.at[c],
            ret_recv.at[e],
            m * flight + c,
        )

    def back_arrival(c):
        return remote(p_v.at[m, band(c)], res_v.at[band(c)], ret_send.at[c], ret_recv.at[c], dev)

    @pl.loop(0, flight)
    def _(j):
        c = mate(j)

        @pl.when(m < last)
        def _():
            taken(m, c).wait_recv()

        @pl.when(m > 0)
        def _():
            taken(SPLIT, c).wait_recv()

        total = p_v[m, band(c), :].astype(F32)
        above = r_v[jnp.where(m < last, m, SPLIT), band(c), :].astype(F32)
        below = r_v[jnp.where(m > 0, SPLIT, m), band(c), :].astype(F32)
        both = jnp.where((m > 0) & (m < last), 1.0, 0.0)
        total = (total + above + both * below).astype(BF16)
        p_v[m, band(c), :] = total

        @pl.when(j > 0)
        def _():
            back(c).start()

    keep = pltpu.make_async_copy(p_v.at[m, band(e)], res_v.at[band(e)], own_sem.at[1])
    keep.start()
    keep.wait()

    @pl.loop(1, flight)
    def _(j):
        back_arrival(mate(j)).wait_recv()

    @pl.loop(0, width // tile)
    def _(i):
        at = pl.ds(pl.multiple_of(i * tile, tile), tile)
        results = res_v[:, at]
        moe_ref[:, at] = (
            jnp.dot(hi_ref[...], results, preferred_element_type=F32)
            + jnp.dot(lo_ref[...], results, preferred_element_type=F32)
        ).astype(BF16)

    @pl.loop(1, flight)
    def _(j):
        first(j).wait_send()
        back(mate(j)).wait_send()

    @pl.loop(0, SPLIT)
    def _(s):
        @pl.loop(0, flight)
        def _(c):
            @pl.when((m < last) & (s <= m))
            def _():
                pass_on(s, c, True).wait_send()

            @pl.when((m > 0) & (s >= m))
            def _():
                pass_on(s, c, False).wait_send()

            @pl.when(s != m)
            def _():
                give(s, c, False).wait_send()


def shards(flight, hidden, norm_gain, router_weight, expert_ids, gate_weight, up_weight, down_weight):
    rows, width = hidden.shape
    cols = flight * CAP
    slice_width = gate_weight.shape[2]
    vmem = pl.BlockSpec(memory_space=pltpu.VMEM)
    hbm = pl.BlockSpec(memory_space=pl.ANY)
    outgoing, hi, lo = pl.pallas_call(
        functools.partial(route_kernel, flight),
        out_shape=(
            jax.ShapeDtypeStruct((cols, width), BF16),
            jax.ShapeDtypeStruct((rows, cols), BF16),
            jax.ShapeDtypeStruct((rows, cols), BF16),
        ),
        in_specs=[vmem] * 4,
        out_specs=(vmem,) * 3,
    )(hidden, norm_gain.reshape(1, width), router_weight, expert_ids)
    dma = pltpu.SemaphoreType.DMA
    return pl.pallas_call(
        functools.partial(expert_kernel, flight),
        out_shape=jax.ShapeDtypeStruct((rows, width), BF16),
        in_specs=[vmem] * 3 + [hbm] * 3,
        out_specs=vmem,
        scratch_shapes=[
            pltpu.VMEM((width, slice_width), BF16),
            pltpu.VMEM((width, slice_width), BF16),
            pltpu.VMEM((slice_width, width), BF16),
            pltpu.VMEM((cols, slice_width), BF16),
            pltpu.VMEM((SPLIT, cols, width), BF16),
            pltpu.VMEM((SPLIT, cols, width), BF16),
            pltpu.VMEM((SPLIT + 1, cols, width), BF16),
            pltpu.VMEM((cols, width), BF16),
            dma((3,)),
            dma((2,)),
            dma((flight,)),
            dma((flight,)),
            dma((2, SPLIT, flight)),
            dma((SPLIT, flight)),
            dma((SPLIT, flight)),
            dma((SPLIT + 1, flight)),
            dma((flight,)),
            dma((flight,)),
        ],
        compiler_params=pltpu.CompilerParams(collective_id=0, has_side_effects=True),
    )(outgoing, hi, lo, gate_weight, up_weight, down_weight)


def solution(mesh):
    flight = mesh.shape["expert"] // SPLIT
    in_specs = (
        P(("group", "expert"), None),
        P(),
        P(),
        P(("group", "expert"), None),
        P("expert", None, None),
        P("expert", None, None),
        P("expert", None, None),
    )
    out_specs = P(("group", "expert"), None)
    return jax.shard_map(
        functools.partial(shards, flight),
        mesh=mesh,
        in_specs=in_specs,
        out_specs=out_specs,
        check_vma=False,
    )
```

time: 166 us -> 90.6 us (0.55)
  the two profiles are of different devices: /device:TPU:13 before, /device:TPU:0 now
where the time goes in v1:
time: 90.6 us; the launch traced here: 89.3 us
  Pallas kernels  84.3 us (93%)
  local copies, waits for them, and re-layouts  4.99 us (6%)
    pallas_call x1, Pallas kernels, shards(): pl.pallas_call(functools.partial(expert_kernel, flight), out_shape=jax.Sh...  80.6 us
    unnamed x2, local copies, waits for them, and re-layouts  3.69 us
    pallas_call x1, Pallas kernels, shards(): pl.pallas_call(functools.partial(route_kernel, flight), out_shape=(jax.Sh...  3.64 us

profile of v1, /device:TPU:0, one launch (start us, length us, event | category | flops | bytes accessed | tf_op | source)
XLA Modules:
  0.0 89.3 jit_solution(9928487377998314624)
XLA Ops:
  0.0 1.3 %reshape.3.gain_ref = bf16[1,4096]{1,0:T(2,128)(2,1)} reshape(bf16[4096]{0:T(1024)(128)(2,1)} %param.8) | data formatting | bytes 16384 | tf_op jit(solution)/shard_map/reshape | solution.py:368
  1.3 1.4 %copy.8.ids_ref = s32[128,8]{1,0:T(8,128)} copy(s32[128,8]{0,1:T(8,128)} %param.10) | data formatting | bytes 8192 | tf_op args[3]
  2.7 3.6 %shard_map.73 = (bf16[64,4096]{1,0:T(8,128)(2,1)}, bf16[128,64]{1,0:T(8,128)(2,1)}, bf16[128,64]{1,0:T(8,128)(2,1)}) custom-call(bf16[128,4096]{1,0:T(8,128)(2,1)} %hidden_ref.1, bf16[1,4096]{1,0:T(2,128)(2,1)} %reshape.3.gain_ref, bf16[4096,128]{1,0:T(8,128)(2,1)} %router_ref.1, s32[128,8]{1,0:T(8,128)} %copy.8.ids_ref), custom_call_target="tpu_custom_call" | custom-call | tf_op jit(solution)/shard_map/pallas_call | solution.py:359
  6.3 80.6 %shard_map.74 = bf16[128,4096]{1,0:T(8,128)(2,1)} custom-call(bf16[64,4096]{1,0:T(8,128)(2,1)} %get-tuple-element.8.out_ref, bf16[128,64]{1,0:T(8,128)(2,1)} %get-tuple-element.9.hi_ref, bf16[128,64]{1,0:T(8,128)(2,1)} %get-tuple-element.10.lo_ref, bf16[1,4096,384]{2,1,0:T(8,128)(2,1)} %gate_hbm.1, bf16[1,4096,384]{2,1,0:T(8,128)(2,1)} %up_hbm.1, ...), custom_call_target="tpu_custom_call" | custom-call | tf_op jit(solution)/shard_map/pallas_call | solution.py:370
  87.0 2.3 %copy.10 = bf16[128,4096]{1,0:T(8,128)(2,1)} copy(bf16[128,4096]{1,0:T(8,128)(2,1)} %shard_map.74) | data formatting | bytes 2097152

commit v2 on v1

--- a/solution.py
+++ b/solution.py
@@ -19,15 +19,16 @@
     cols = flight * CAP
     widened = hidden_ref[...].astype(F32)
     inv_rms = lax.rsqrt(jnp.mean(widened * widened, axis=-1, keepdims=True) + 1e-06)
-    normed = (widened * inv_rms * gain_ref[...].astype(F32)).astype(BF16)
+    normed = (widened * inv_rms * gain_ref[...].astype(F32)[None, :]).astype(BF16)
     logits = jnp.dot(normed, router_ref[...], preferred_element_type=F32)
     shifted = jnp.exp(logits - jnp.max(logits, axis=-1, keepdims=True))
     probs = shifted / jnp.sum(shifted, axis=-1, keepdims=True)
     ids = ids_ref[...]
-    expert = lax.broadcasted_iota(jnp.int32, (rows, experts), 1)
-    chosen = jnp.zeros((rows, experts), F32)
-    for k in range(ids.shape[1]):
-        chosen = jnp.where(ids[:, k : k + 1] == expert, 1.0, chosen)
+    expert = lax.broadcasted_iota(jnp.int32, (experts, rows), 0)
+    chosen = jnp.zeros((experts, rows), F32)
+    for k in range(ids.shape[0]):
+        chosen = jnp.where(ids[k : k + 1, :] == expert, 1.0, chosen)
+    chosen = chosen.T
     picked = probs * chosen
     share = picked / jnp.sum(picked, axis=-1, keepdims=True)
     chosen_b = chosen.astype(BF16)
@@ -142,16 +143,16 @@
         c = mate(j)
         return remote(
             out_ref.at[band(c)],
-            x_v.at[m, band(e)],
-            p1_send.at[c],
-            p1_recv.at[e],
+            x_v.at[m, band(j)],
+            p1_send.at[j],
+            p1_recv.at[j],
             m * flight + c,
         )
 
-    def first_arrival(c):
-        return remote(out_ref.at[band(c)], x_v.at[m, band(c)], p1_send.at[c], p1_recv.at[c], dev)
-
-    own = pltpu.make_async_copy(out_ref.at[band(e)], x_v.at[m, band(e)], own_sem.at[0])
+    def first_arrival(j):
+        return remote(out_ref.at[band(j)], x_v.at[m, band(j)], p1_send.at[j], p1_recv.at[j], dev)
+
+    own = pltpu.make_async_copy(out_ref.at[band(e)], x_v.at[m, band(0)], own_sem.at[0])
     own.start()
 
     @pl.loop(1, flight)
@@ -178,13 +179,12 @@
             pass_on(s, c, False).start()
 
     own.wait()
-    spread(m, e)
+    spread(m, 0)
 
     @pl.loop(1, flight)
     def _(j):
-        c = mate(flight - j)
-        first_arrival(c).wait_recv()
-        spread(m, c)
+        first_arrival(j).wait_recv()
+        spread(m, j)
 
     for copy in weights:
         copy.wait()
@@ -205,20 +205,40 @@
             r_v.at[slot, band(c)], r_v.at[slot, band(c)], rs_send.at[0, c], rs_recv.at[slot, c], dev
         )
 
-    def compute(s):
-        rows = x_v[s]
+    def compute(s, start, count):
+        here = pl.ds(start, count)
+        rows = x_v[s, here, :]
         gate = jnp.dot(rows, gate_v[...], preferred_element_type=F32)
         up = jnp.dot(rows, up_v[...], preferred_element_type=F32)
-        act_v[...] = (jax.nn.silu(gate) * up).astype(BF16)
+        act_v[here, :] = (jax.nn.silu(gate) * up).astype(BF16)
 
         @pl.loop(0, width // tile)
         def _(i):
             at = pl.ds(pl.multiple_of(i * tile, tile), tile)
-            p_v[s, :, at] = jnp.dot(
-                act_v[...], down_v[:, at], preferred_element_type=F32
+            p_v[s, here, at] = jnp.dot(
+                act_v[here, :], down_v[:, at], preferred_element_type=F32
             ).astype(BF16)
 
-    @pl.loop(0, SPLIT)
+    def arrive(s, begin, end):
+        @pl.loop(begin, end)
+        def _(c):
+            pass_on(s, c, True).wait_recv()
+            spread(s, c)
+
+    def begin_sums(s, begin, end):
+        @pl.when((s < m) & (m == last))
+        def _():
+            @pl.loop(begin, end)
+            def _(c):
+                give(s, c, False).start()
+
+        @pl.when((s > m) & (m == 0))
+        def _():
+            @pl.loop(begin, end)
+            def _(c):
+                give(s, c, True).start()
+
+    @pl.loop(0, last)
     def _(t):
         @pl.loop(0, 2)
         def _(d):
@@ -226,10 +246,7 @@
 
             @pl.when((t > 0) & (s >= 0) & (s <= last))
             def _():
-                @pl.loop(0, flight)
-                def _(c):
-                    pass_on(s, c, True).wait_recv()
-                    spread(s, c)
+                arrive(s, 0, flight)
 
         @pl.loop(0, 2)
         def _(d):
@@ -237,19 +254,21 @@
 
             @pl.when((s >= 0) & (s <= last) & ((t > 0) | (d == 0)))
             def _():
-                compute(s)
-
-                @pl.when((s < m) & (m == last))
-                def _():
-                    @pl.loop(0, flight)
-                    def _(c):
-                        give(s, c, False).start()
-
-                @pl.when((s > m) & (m == 0))
-                def _():
-                    @pl.loop(0, flight)
-                    def _(c):
-                        give(s, c, True).start()
+                compute(s, 0, flight * CAP)
+                begin_sums(s, 0, flight)
+
+    pieces = 2 if flight % 2 == 0 else 1
+    step = flight // pieces
+
+    @pl.when((m == 0) | (m == last))
+    def _():
+        far = last - m
+
+        @pl.loop(0, pieces)
+        def _(h):
+            arrive(far, h * step, (h + 1) * step)
+            compute(far, pl.multiple_of(h * step * CAP, step * CAP), step * CAP)
+            begin_sums(far, h * step, (h + 1) * step)
 
     def add(s, slot, c):
         taken(slot, c).wait_recv()
@@ -276,22 +295,20 @@
                 add(rise, rise, c)
                 give(rise, c, True).start()
 
-    def back(c):
+    def back(j):
         return remote(
-            p_v.at[m, band(c)],
+            p_v.at[m, band(j)],
             res_v.at[band(e)],
-            ret_send.at[c],
+            ret_send.at[j],
             ret_recv.at[e],
-            m * flight + c,
+            m * flight + mate(flight - j),
         )
 
     def back_arrival(c):
         return remote(p_v.at[m, band(c)], res_v.at[band(c)], ret_send.at[c], ret_recv.at[c], dev)
 
     @pl.loop(0, flight)
-    def _(j):
-        c = mate(j)
-
+    def _(c):
         @pl.when(m < last)
         def _():
             taken(m, c).wait_recv()
@@ -307,11 +324,11 @@
         total = (total + above + both * below).astype(BF16)
         p_v[m, band(c), :] = total
 
-        @pl.when(j > 0)
+        @pl.when(c > 0)
         def _():
             back(c).start()
 
-    keep = pltpu.make_async_copy(p_v.at[m, band(e)], res_v.at[band(e)], own_sem.at[1])
+    keep = pltpu.make_async_copy(p_v.at[m, band(0)], res_v.at[band(e)], own_sem.at[1])
     keep.start()
     keep.wait()
 
@@ -331,7 +348,7 @@
     @pl.loop(1, flight)
     def _(j):
         first(j).wait_send()
-        back(mate(j)).wait_send()
+        back(j).wait_send()
 
     @pl.loop(0, SPLIT)
     def _(s):
@@ -365,7 +382,7 @@
         ),
         in_specs=[vmem] * 4,
         out_specs=(vmem,) * 3,
-    )(hidden, norm_gain.reshape(1, width), router_weight, expert_ids)
+    )(hidden, norm_gain, router_weight, expert_ids.T)
     dma = pltpu.SemaphoreType.DMA
     return pl.pallas_call(
         functools.partial(expert_kernel, flight),

time: 90.6 us -> 84.4 us (0.932); the launches traced: 89.3 us -> 84.2 us
  local copies, waits for them, and re-layouts: 4.99 us -> 2.29 us
  Pallas kernels: 84.3 us -> 81.9 us
    pallas_call x1, Pallas kernels: 80.6 us -> 78.3 us  [shards(): pl.pallas_call(functools.partial(expert_kernel, flight), out_shape=jax.Sh...]
    unnamed x2 -> x1, local copies, waits for them, and re-layouts: 3.69 us -> 2.29 us
    reshape x1 -> x0, local copies, waits for them, and re-layouts: 1.3 us -> none  [shards(): norm_gain.reshape(1, width)]
where the time goes in v2:
time: 84.4 us; the launch traced here: 84.2 us
  Pallas kernels  81.9 us (97%)
  local copies, waits for them, and re-layouts  2.29 us (3%)
    pallas_call x1, Pallas kernels, shards(): pl.pallas_call(functools.partial(expert_kernel, flight), out_shape=jax.Sh...  78.3 us
    pallas_call x1, Pallas kernels, shards(): pl.pallas_call(functools.partial(route_kernel, flight), out_shape=(jax.Sh...  3.61 us
    unnamed x1, local copies, waits for them, and re-layouts  2.29 us

profile of v2, /device:TPU:0, one launch (start us, length us, event | category | flops | bytes accessed | tf_op | source)
XLA Modules:
  0.0 84.2 jit_solution(14542087614362527594)
XLA Ops:
  0.0 3.6 %shard_map.73 = (bf16[64,4096]{1,0:T(8,128)(2,1)}, bf16[128,64]{1,0:T(8,128)(2,1)}, bf16[128,64]{1,0:T(8,128)(2,1)}) custom-call(bf16[128,4096]{1,0:T(8,128)(2,1)} %hidden_ref.1, bf16[4096]{0:T(1024)(128)(2,1)} %gain_ref.1, bf16[4096,128]{1,0:T(8,128)(2,1)} %router_ref.1, s32[8,128]{1,0:T(8,128)} %bitcast.1), custom_call_target="tpu_custom_call" | custom-call | tf_op jit(solution)/shard_map/pallas_call | solution.py:376
  3.6 78.3 %shard_map.74 = bf16[128,4096]{1,0:T(8,128)(2,1)} custom-call(bf16[64,4096]{1,0:T(8,128)(2,1)} %get-tuple-element.8.out_ref, bf16[128,64]{1,0:T(8,128)(2,1)} %get-tuple-element.9.hi_ref, bf16[128,64]{1,0:T(8,128)(2,1)} %get-tuple-element.10.lo_ref, bf16[1,4096,384]{2,1,0:T(8,128)(2,1)} %gate_hbm.1, bf16[1,4096,384]{2,1,0:T(8,128)(2,1)} %up_hbm.1, ...), custom_call_target="tpu_custom_call" | custom-call | tf_op jit(solution)/shard_map/pallas_call | solution.py:387
  81.9 2.3 %copy.9 = bf16[128,4096]{1,0:T(8,128)(2,1)} copy(bf16[128,4096]{1,0:T(8,128)(2,1)} %shard_map.74) | data formatting | bytes 2097152
